TPU v7x, 32 devices: a whole 2x2x4 slice. The times are simulated.
32 devices in a mesh: row: 4 (over y, x), col: 8 (over z, core).
Axes of the slice: x: 2, y: 2, z: 4, core: 2. Of those that a mesh axis runs over, the one named last changes fastest.
Arguments:
- tokens: bfloat16 [512, 7168], P('col', 'row'), may hold values from -6 to 6
- routes: int32 [512, 8], P('col'), may hold values from 0 to 15, all different within a row; in each aligned block of 64 rows (0 to 63, 64 to 127, ...) at most 40 rows name the same one
- gates: float32 [512, 8], P('col'), may hold values from 0.05 to 0.5
- w_gate: bfloat16 [16, 7168, 2048], P('col', None, 'row'), may hold values from -0.0625 to 0.0625
- w_up: bfloat16 [16, 7168, 2048], P('col', None, 'row'), may hold values from -0.0625 to 0.0625
- w_down: bfloat16 [16, 2048, 7168], P('col', 'row'), may hold values from -0.125 to 0.125
Outputs:
- mixed: bfloat16 [512, 7168], P('col', 'row')
Inputs may be any that keep to these rules, and one draw needn't show every extreme that they name: `routes`: the 8 experts of a token are distinct. Among the 64 tokens of one index of col (aligned blocks of 64 tokens), no expert is chosen more than 40 times, and some expert is chosen exactly 40 times.
All inputs are finite; a program needn't handle non-finite values.
Results may differ from a plain program's by a relative error of at most 0.015.
Values may be sent and summed in bfloat16 or wider, within the bound.
A program may use at most 128 MiB of HBM per device.

v0:
```python
import jax
import jax.numpy as jnp
from jax import lax
from jax.sharding import PartitionSpec as P

CAP = 40


def group_positions(grouped, expert_count):
    onehot = (
        grouped[:, :, None] == jnp.arange(expert_count, dtype=jnp.int32)[None, None, :]
    ).astype(jnp.int32)
    before = jnp.cumsum(onehot, axis=1) - onehot
    return jnp.sum(before * onehot, axis=2)


def shards(tokens, routes, gates, w_gate, w_up, w_down):
    held_experts = w_gate.shape[0]
    group_count = lax.axis_size("col")
    expert_count = held_experts * group_count
    tok_rows, top_count = routes.shape
    flat_routes = routes.reshape(1, tok_rows * top_count)
    position = group_positions(flat_routes, expert_count)[0]
    target = flat_routes[0] * CAP + position
    owner_rows = jnp.arange(tok_rows * top_count, dtype=jnp.int32) // top_count
    outgoing = jnp.zeros((expert_count * CAP, tokens.shape[1]), jnp.bfloat16)
    outgoing = (
        outgoing.at[target].set(tokens[owner_rows]).reshape(expert_count, CAP, tokens.shape[1])
    )
    arrived = lax.all_to_all(outgoing, "col", split_axis=0, concat_axis=1, tiled=True)
    piece = lax.all_gather(arrived, "row", axis=2, tiled=True)
    gate_act = jnp.einsum("erd,edf->erf", piece, w_gate, preferred_element_type=jnp.float32)
    up_act = jnp.einsum("erd,edf->erf", piece, w_up, preferred_element_type=jnp.float32)
    hidden = (jax.nn.silu(gate_act) * up_act).astype(jnp.bfloat16)
    term_sum = jnp.einsum("erf,efd->erd", hidden, w_down, preferred_element_type=jnp.float32)
    result = lax.psum_scatter(term_sum.astype(jnp.bfloat16), "row", scatter_dimension=2, tiled=True)
    returned = lax.all_to_all(result, "col", split_axis=1, concat_axis=0, tiled=True)
    picked = returned.reshape(expert_count * CAP, returned.shape[2])[target]
    picked = picked.reshape(tok_rows, top_count, returned.shape[2])
    mixed = jnp.sum(gates[:, :, None] * picked.astype(jnp.float32), axis=1)
    return mixed.astype(jnp.bfloat16)


def solution(mesh):
    return jax.shard_map(
        shards,
        mesh=mesh,
        in_specs=(
            P("col", "row"),
            P("col", None),
            P("col", None),
            P("col", None, "row"),
            P("col", None, "row"),
            P("col", "row", None),
        ),
        out_specs=P("col", "row"),
        check_vma=False,
    )
```

profile of v0, /device:TPU:0, one launch (start us, length us, event | category | flops | bytes accessed | tf_op | source)
XLA Modules:
  0.0 383.8 jit_solution(356704290422675333)
XLA Ops:
  6.5 0.0 copy-start
  6.5 0.0 all-gather.2.cloned.1.call-start
  6.5 0.8 copy.19
  7.4 0.1 eq.27
  7.5 1.2 reduce-window.6
  8.6 0.2 slice_reduce_fusion
  8.9 0.7 broadcast_multiply_fusion
  9.6 0.1 copy.22
  9.7 0.1 copy.18
  9.8 0.1 mul.37
  9.9 0.1 broadcast.138
  10.0 0.1 fusion.5
  10.1 0.0 copy-done
  10.1 9.9 %scatter_custom_fusion = bf16[640,1792]{1,0:T(8,128)(2,1)S(1)} fusion(s32[512]{0:T(512)S(1)} %bitcast.43, bf16[64,1792]{1,0:T(8,128)(2,1)S(1)} %copy-done, s32[1024]{0:T(1024)S(1)} %pad_clamp_fusion.1, bf16[]{:T(256)} %constant.26.clone.1), kind=kCustom, calls=%fused_computation.6 | custom fusion | bytes 2293762 | tf_op jit(solution)/shard_map/scatter | solution.py:28
  20.0 59.4 %all_to_all.33 = bf16[16,40,1792]{2,1,0:T(8,128)(2,1)S(1)} all-to-all(bf16[16,40,1792]{2,1,0:T(8,128)(2,1)S(1)} %bitcast.38), channel_id=1, replica_groups=mesh['row'=4,'col'=8] {'col'}, dimensions={0} | all-to-all | bytes 4587520 | tf_op jit(solution)/shard_map/all_to_all | solution.py:30
  79.4 1.6 copy.23
  80.9 0.0 all-gather.2.cloned.1.call-update
  80.9 0.2 reduce-scatter.2.cloned.1.call-start
  81.2 92.9 %all-gather.2.cloned.1.call-done = bf16[2,320,7168]{2,1,0:T(8,128)(2,1)} async-done(((bf16[2,320,1792]{2,1,0:T(8,128)(2,1)}), bf16[2,320,7168]{2,1,0:T(8,128)(2,1)}) %all-gather.2.cloned.1.call-update) | async-done | bytes 9175056 | tf_op jit(solution)/shard_map/all_gather | solution.py:31
  174.1 10.8 %fusion.6 = f32[2,320,512]{2,1,0:T(8,128)S(1)} fusion(bf16[2,320,7168]{2,1,0:T(8,128)(2,1)} %all-gather.2.cloned.1.call-done, bf16[2,7168,512]{2,1,0:T(8,128)(2,1)} %param.9), kind=kOutput, calls=%fused_computation.26 | convolution fusion | flops 4697620480 | bytes 25165824 | tf_op jit(solution)/shard_map/erd,edf->erf/dot_general | solution.py:32
  184.9 12.7 %fusion.3 = bf16[2,320,512]{2,1,0:T(8,128)(2,1)S(1)} fusion(bf16[2,320,7168]{2,1,0:T(8,128)(2,1)} %all-gather.2.cloned.1.call-done, bf16[2,7168,512]{2,1,0:T(8,128)(2,1)} %param.10, f32[2,320,512]{2,1,0:T(8,128)S(1)} %fusion.6), kind=kOutput, calls=%fused_computation.9 | convolution fusion | flops 4699586560 | bytes 25821184 | tf_op jit(solution)/shard_map/erd,edf->erf/dot_general | solution.py:33
  197.6 12.7 %convolution_convert_fusion = bf16[2,320,7168]{2,1,0:T(8,128)(2,1)} fusion(bf16[2,320,512]{2,1,0:T(8,128)(2,1)S(1)} %fusion.3, bf16[2,512,7168]{2,1,0:T(8,128)(2,1)} %param.11), kind=kOutput, calls=%fused_computation.3 | convolution fusion | flops 4702208000 | bytes 24510464 | tf_op jit(solution)/shard_map/erf,efd->erd/dot_general | solution.py:35
  210.4 0.0 reduce-scatter.2.cloned.1.call-update
  210.4 92.9 %reduce-scatter.2.cloned.1.call-done = bf16[2,320,1792]{2,1,0:T(8,128)(2,1)} async-done(((bf16[2,320,7168]{2,1,0:T(8,128)(2,1)}), bf16[2,320,1792]{2,1,0:T(8,128)(2,1)}) %reduce-scatter.2.cloned.1.call-update) | async-done | bytes 2293776 | tf_op jit(solution)/shard_map/reduce_scatter | solution.py:36
  303.3 5.4 %copy.24 = bf16[2,320,1792]{2,0,1:T(2,128)(2,1)} copy(bf16[2,320,1792]{2,1,0:T(8,128)(2,1)} %reduce-scatter.2.cloned.1.call-done) | data formatting | bytes 4587520 | tf_op jit(solution)/shard_map/reduce_scatter | solution.py:36
  308.7 0.0 copy-start.3
  308.7 4.7 %all-to-all-start.1 = ((bf16[2,320,1792]{2,0,1:T(2,128)(2,1)}), bf16[2,320,1792]{2,0,1:T(2,128)(2,1)S(1)}, u32[]{:S(2)}, u32[]{:S(2)}) async-start(bf16[2,320,1792]{2,0,1:T(2,128)(2,1)} %copy.24), calls=%async_computation.2 | async-start | bytes 4587520 | tf_op jit(solution)/shard_map/all_to_all | solution.py:37
  313.4 0.0 copy-done.3
  313.4 0.1 copy.17
  313.5 53.2 %all-to-all-done.1 = bf16[2,320,1792]{2,0,1:T(2,128)(2,1)S(1)} async-done(((bf16[2,320,1792]{2,0,1:T(2,128)(2,1)}), bf16[2,320,1792]{2,0,1:T(2,128)(2,1)S(1)}, u32[]{:S(2)}, u32[]{:S(2)}) %all-to-all-start.1) | async-done | bytes 2293792 | tf_op jit(solution)/shard_map/all_to_all | solution.py:37
  366.7 0.0 copy-start.2
  366.7 1.4 copy-done.2
  368.1 1.9 copy.25
  369.9 0.0 copy-start.1
  369.9 3.2 gather_fusion
  373.1 3.8 fusion
  376.9 0.0 copy-done.1
  (9 shorter events, 0.1 us)
Async XLA Ops:
  6.5 3.5 copy-start
  6.5 167.5 %all-gather.2.cloned.1.call-start = ((), (), s32[]{:S(2)}) async-start(), calls=%async_computation.3 | async-start | bytes 11468800 | tf_op jit(solution)/shard_map/all_gather | solution.py:31
  80.9 222.3 %reduce-scatter.2.cloned.1.call-start = ((), (), s32[]{:S(2)}) async-start(), calls=%async_computation.4 | async-start | bytes 11468800 | tf_op jit(solution)/shard_map/reduce_scatter | solution.py:36
  308.7 4.7 %copy-start.3 = (f32[64,8]{0,1:T(8,128)S(1)}, f32[64,8]{0,1:T(8,128)}, u32[]{:S(2)}) copy-start(f32[64,8]{0,1:T(8,128)} %param.8) | copy-start | bytes 6148
  308.7 58.0 %all-to-all-start.1 = ((bf16[2,320,1792]{2,0,1:T(2,128)(2,1)}), bf16[2,320,1792]{2,0,1:T(2,128)(2,1)S(1)}, u32[]{:S(2)}, u32[]{:S(2)}) async-start(bf16[2,320,1792]{2,0,1:T(2,128)(2,1)} %copy.24), calls=%async_computation.2 | async-start | bytes 4587520 | tf_op jit(solution)/shard_map/all_to_all | solution.py:37
  366.7 1.4 copy-start.2
  369.9 7.0 %copy-start.1 = (bf16[64,1792]{1,0:T(8,128)(2,1)S(1)}, bf16[64,1792]{1,0:T(8,128)(2,1)}, u32[]{:S(2)}) copy-start(bf16[64,1792]{1,0:T(8,128)(2,1)} %param.6) | copy-start | bytes 688132
Sparse Core Ops, SparseCore 0:
  81.1 92.9 all-gather.1
  210.5 92.7 reduce-scatter.1
where the time goes:
time: 384 us
  waiting for transfers between devices  239 us (62%)
  blocking collectives  59.4 us (15%)
  matrix products  36.3 us (9%)
  local copies, waits for them, and re-layouts  24.8 us (6%)
  between operations  13.5 us (4%)
  other arithmetic  5.83 us (2%)
  starting transfers between devices  4.96 us (1%)
    reduce_scatter x1, waiting for transfers between devices, shards(): lax.psum_scatter(term_sum.astype(jnp.bfloat16), 'row', scatter_dimension=...  92.9 us
    all_gather x1, waiting for transfers between devices, shards(): piece = lax.all_gather(arrived, 'row', axis=2, tiled=True)  92.9 us
    all_to_all x1, blocking collectives, shards(): lax.all_to_all(outgoing, 'col', split_axis=0, concat_axis=1, tiled=True)  59.4 us
    all_to_all x1, waiting for transfers between devices, shards(): lax.all_to_all(result, 'col', split_axis=1, concat_axis=0, tiled=True)  53.2 us
    dot_general x1, matrix products, shards(): jnp.einsum('erd,edf->erf', piece, w_up, preferred_element_type=jnp.float32)  12.7 us
    dot_general x1, matrix products, shards(): jnp.einsum('erf,efd->erd', hidden, w_down, preferred_element_type=jnp.flo...  12.7 us
    dot_general x1, matrix products, shards(): jnp.einsum('erd,edf->erf', piece, w_gate, preferred_element_type=jnp.floa...  10.8 us
    scatter x1, local copies, waits for them, and re-layouts, shards(): outgoing.at[target].set(tokens[owner_rows])  9.86 us
  transfers between devices with their start and end apart: 3, of which 3 were waited for; matrix products, arithmetic and copies ran while one was open for 0% of the time, Pallas kernels for 0%

commit v1 on v0

v1 whole, which is shorter than its diff:
```python
import functools
import math

import jax
import jax.numpy as jnp
from jax import lax
from jax.experimental import pallas as pl
from jax.experimental.pallas import tpu as pltpu
from jax.sharding import PartitionSpec as P

MESH = pl.DeviceIdType.MESH
LANES = 128


def flip(value, mask):
    bit = 1
    while bit <= mask:
        if mask & bit:
            value = value + bit - 2 * bit * lax.rem(lax.div(value, bit), 2)
        bit *= 2
    return value


def kernel(
    side, depth, tokens, routes, gates, w_gate, w_up, w_down, out,
    x_all, g_all, w_buf, wd, acc, hid, part, pair, dx_in, dy_in, rx_in, ry_in, z_in,
    z_s, z_r, gz_s, gz_r, gp_s, gp_r, x_s, x_r, y_s, y_r, du_s, du_r, dl_s, dl_r,
    p_s, p_r, w_sem, wd_sem, own_sem,
    q_s, q_r, ou_s, ou_r, ol_s, ol_r, rx_s, rx_r, ry_s, ry_r, oz_s, oz_r,
):
    rows, feat = tokens.shape
    held, _, width = w_gate.shape
    half = rows // 2
    row, col = lax.axis_index("row"), lax.axis_index("col")
    yy, xx = lax.div(row, side), lax.rem(row, side)
    zz, core = lax.div(col, 2), lax.rem(col, 2)
    far = range(1, side)
    levels = range(depth)

    def row_of(dy, dx):
        return flip(yy, dy) * side + flip(xx, dx)

    def spot(j, plane=None):
        return (core if plane is None else plane) * depth + flip(zz, j)

    partner = (row, zz * 2 + 1 - core)

    def x_dev(dx):
        return (row_of(0, dx), col)

    def y_dev(dy):
        return (row_of(dy, 0), col)

    def z_dev(j):
        return (row, flip(zz, j) * 2 + core)

    sent = []

    def copy_of(src, dst, ss, rs, dev):
        return pltpu.make_async_remote_copy(
            src_ref=src, dst_ref=dst, send_sem=ss, recv_sem=rs,
            device_id=dev, device_id_type=MESH,
        )

    def send(src, dst, ss, rs, dev):
        copy = copy_of(src, dst, ss, rs, dev)
        copy.start()
        sent.append(copy)

    def arrive(ref, ss, rs):
        copy_of(ref, ref, ss, rs, partner).wait_recv()

    order = [(dy, dx) for dy in range(side) for dx in range(side)]
    per = 2 * held
    slots = w_buf.shape[0]
    units = len(order) * per

    def fetch(u):
        s, i = divmod(u, per)
        e, m = divmod(i, 2)
        start = pl.multiple_of(row_of(*order[s]) * feat, LANES)
        return pltpu.make_async_copy(
            (w_up if m else w_gate).at[e, pl.ds(start, feat), :],
            w_buf.at[u % slots],
            w_sem.at[u % slots],
        )

    for u in range(min(slots, units)):
        fetch(u).start()
    own = pltpu.make_async_copy(tokens, x_all.at[row, spot(0)], own_sem)
    own.start()

    lane = lax.broadcasted_iota(jnp.int32, (rows, LANES), 1)
    dense = jnp.zeros((rows, LANES), jnp.float32)
    for k in range(routes.shape[1]):
        dense = dense + jnp.where(lane == routes[:, k : k + 1], gates[:, k : k + 1], 0.0)
    g_all[spot(0)] = dense

    barrier = pltpu.get_barrier_semaphore()
    peers = [partner] + [x_dev(d) for d in far] + [y_dev(d) for d in far]
    peers += [z_dev(j) for j in levels[1:]]
    for peer in peers:
        pl.semaphore_signal(barrier, inc=1, device_id=peer, device_id_type=MESH)
    pl.semaphore_wait(barrier, len(peers))

    mine = x_all.at[row, spot(0)]
    for d in far:
        send(tokens, mine, x_s.at[d - 1, 0], x_r.at[d - 1, 0], x_dev(d))
        send(tokens, mine, y_s.at[d - 1, 0], y_r.at[d - 1, 0], y_dev(d))
    for j in levels[1:]:
        send(tokens, mine, z_s.at[j], z_r.at[j], z_dev(j))
    send(tokens, mine, p_s.at[0, 0, 0], p_r.at[0, 0, 0], partner)
    for j in levels[1:]:
        send(g_all.at[spot(0)], g_all.at[spot(0)], gz_s.at[j], gz_r.at[j], z_dev(j))
    send(g_all.at[spot(0)], g_all.at[spot(0)], gp_s.at[0], gp_r.at[0], partner)
    downs = [
        pltpu.make_async_copy(w_down.at[e], wd.at[pl.ds(e * width, width), :], wd_sem.at[e])
        for e in range(held)
    ]
    for down in downs:
        down.start()
    acc[...] = jnp.zeros_like(acc)
    own.wait()

    def block(dy, dx, j):
        return x_all.at[row_of(dy, dx), spot(j)]

    def share(dy, dx, j):
        ref = block(dy, dx, j)
        send(ref, ref, p_s.at[dy, dx, j], p_r.at[dy, dx, j], partner)

    def z_event(j):
        ref = block(0, 0, j)
        arrive(ref, z_s.at[j], z_r.at[j])
        for d in far:
            send(ref, ref, x_s.at[d - 1, j], x_r.at[d - 1, j], x_dev(d))
            send(ref, ref, y_s.at[d - 1, j], y_r.at[d - 1, j], y_dev(d))
        share(0, 0, j)

    def xy_event(j):
        for d in far:
            ref = block(0, d, j)
            arrive(ref, x_s.at[d - 1, j], x_r.at[d - 1, j])
            top = ref.at[pl.ds(0, half)]
            for v in far:
                send(top, top, du_s.at[v - 1, d - 1, j], du_r.at[v - 1, d - 1, j], y_dev(v))
            share(0, d, j)
            ref = block(d, 0, j)
            arrive(ref, y_s.at[d - 1, j], y_r.at[d - 1, j])
            low = ref.at[pl.ds(half, half)]
            for v in far:
                send(low, low, dl_s.at[d - 1, v - 1, j], dl_r.at[d - 1, v - 1, j], x_dev(v))
            share(d, 0, j)

    def diag_event(j):
        for v in far:
            for d in far:
                ref = block(v, d, j)
                at = (v - 1, d - 1, j)
                arrive(ref.at[pl.ds(0, half)], du_s.at[at], du_r.at[at])
                arrive(ref.at[pl.ds(half, half)], dl_s.at[at], dl_r.at[at])
                share(v, d, j)

    def gate_event(j):
        ref = g_all.at[spot(j)]
        arrive(ref, gz_s.at[j], gz_r.at[j])
        send(ref, ref, gp_s.at[j], gp_r.at[j], partner)

    def ready(dy, dx):
        for j in levels:
            arrive(
                x_all.at[row_of(dy, dx), spot(j, 1 - core)], p_s.at[dy, dx, j], p_r.at[dy, dx, j]
            )

    def multiply(u):
        s, i = divmod(u, per)
        fetch(u).wait()
        left = x_all[row_of(*order[s])].reshape(2 * depth * rows, feat)
        acc[i] += jnp.dot(left, w_buf[u % slots], preferred_element_type=jnp.float32)
        if u + slots < units:
            fetch(u + slots).start()

    events = []
    for j in range(1, depth):
        events.append(functools.partial(z_event, j))
        events.append(functools.partial(xy_event, j - 1))
        if j >= 2:
            events.append(functools.partial(diag_event, j - 2))
    for event in events:
        event()
    for j in levels[1:]:
        gate_event(j)
    late = [functools.partial(xy_event, depth - 1)]
    late += [functools.partial(diag_event, j) for j in range(max(depth - 2, 0), depth)]
    stand = {per // 2: late[:1], 2 * per: late[1:2], 2 * per + per // 2: late[2:3]}
    ready(0, 0)
    for u in range(units):
        for event in stand.get(u, []):
            event()
        if u % per == 0 and u:
            ready(*order[u // per])
        multiply(u)

    for j in levels:
        arrive(g_all.at[spot(j, 1 - core)], gp_s.at[j], gp_r.at[j])

    def activate(b, _):
        at = pl.ds(pl.multiple_of(b * rows, rows), rows)
        for e in range(held):
            weight = jnp.sum(
                jnp.where(lane == col * held + e, g_all[b], 0.0), axis=1, keepdims=True
            )
            a, u = acc[2 * e, at, :], acc[2 * e + 1, at, :]
            value = a / (1.0 + jnp.exp(-a)) * u * weight
            hid[at, e * width : (e + 1) * width] = value.astype(jnp.bfloat16)
        return 0

    lax.fori_loop(0, 2 * depth, activate, 0)
    for down in downs:
        down.wait()

    def project(dy, dx, plane):
        rid = row_of(dy, dx)
        at = pl.ds(pl.multiple_of(plane * (depth * rows), rows), depth * rows)
        cols = pl.ds(pl.multiple_of(rid * feat, LANES), feat)
        value = jnp.dot(hid[at, :], wd[:, cols], preferred_element_type=jnp.float32)
        part[rid, pl.ds(plane * depth, depth)] = value.astype(jnp.bfloat16).reshape(
            depth, rows, feat
        )

    def swap(dy, dx):
        rid = row_of(dy, dx)
        send(
            part.at[rid, pl.ds((1 - core) * depth, depth)], pair.at[rid],
            q_s.at[dy, dx], q_r.at[dy, dx], partner,
        )

    def paired(dy, dx):
        arrive(pair.at[row_of(dy, dx)], q_s.at[dy, dx], q_r.at[dy, dx])

    def f32(value):
        return value.astype(jnp.float32)

    def both(dy, dx, j):
        rid = row_of(dy, dx)
        return f32(part[rid, spot(j)]) + f32(pair[rid, flip(zz, j)])

    back = [(v, d) for v in far for d in far]
    sides = [(0, d) for d in far] + [(d, 0) for d in far]
    falling = list(reversed(levels))

    def diag_out():
        for v, d in back:
            paired(v, d)
            for j in falling:
                ref = part.at[row_of(v, d), spot(j)]
                part[row_of(v, d), spot(j)] = both(v, d, j).astype(jnp.bfloat16)
                at = (v - 1, d - 1, j)
                send(ref.at[pl.ds(0, half)], dx_in.at[at], ou_s.at[at], ou_r.at[at], x_dev(d))
                send(ref.at[pl.ds(half, half)], dy_in.at[at], ol_s.at[at], ol_r.at[at], y_dev(v))

    todo = back + sides + [(0, 0)]
    for n, (dy, dx) in enumerate(todo):
        project(dy, dx, 1 - core)
        swap(dy, dx)
        if n == len(back):
            diag_out()
        project(dy, dx, core)

    for dy, dx in sides:
        paired(dy, dx)
    for j in falling:
        for d in far:
            total = both(0, d, j)
            top, low = total[:half], total[half:]
            for v in far:
                at = (v - 1, d - 1, j)
                arrive(dy_in.at[at], ol_s.at[at], ol_r.at[at])
                low = low + f32(dy_in[at])
            ref = part.at[row_of(0, d), spot(j)]
            ref[pl.ds(0, half), :] = top.astype(jnp.bfloat16)
            ref[pl.ds(half, half), :] = low.astype(jnp.bfloat16)
            send(ref, rx_in.at[d - 1, j], rx_s.at[d - 1, j], rx_r.at[d - 1, j], x_dev(d))
        for v in far:
            total = both(v, 0, j)
            top, low = total[:half], total[half:]
            for d in far:
                at = (v - 1, d - 1, j)
                arrive(dx_in.at[at], ou_s.at[at], ou_r.at[at])
                top = top + f32(dx_in[at])
            ref = part.at[row_of(v, 0), spot(j)]
            ref[pl.ds(0, half), :] = top.astype(jnp.bfloat16)
            ref[pl.ds(half, half), :] = low.astype(jnp.bfloat16)
            send(ref, ry_in.at[v - 1, j], ry_s.at[v - 1, j], ry_r.at[v - 1, j], y_dev(v))
    paired(0, 0)
    for j in falling:
        total = both(0, 0, j)
        for d in far:
            arrive(rx_in.at[d - 1, j], rx_s.at[d - 1, j], rx_r.at[d - 1, j])
            arrive(ry_in.at[d - 1, j], ry_s.at[d - 1, j], ry_r.at[d - 1, j])
            total = total + f32(rx_in[d - 1, j]) + f32(ry_in[d - 1, j])
        if j:
            ref = part.at[row, spot(j)]
            ref[...] = total.astype(jnp.bfloat16)
            send(ref, z_in.at[j - 1], oz_s.at[j], oz_r.at[j], z_dev(j))
    for j in falling[:-1]:
        arrive(z_in.at[j - 1], oz_s.at[j], oz_r.at[j])
        total = total + f32(z_in[j - 1])
    out[...] = total.astype(jnp.bfloat16)
    for copy in sent:
        copy.wait_send()


def one_kernel(tokens, routes, gates, w_gate, w_up, w_down):
    rows, feat = tokens.shape
    held, dim, width = w_gate.shape
    row_count, col_count = lax.axis_size("row"), lax.axis_size("col")
    side, depth = math.isqrt(row_count), col_count // 2
    f, half, bf, ff = side - 1, rows // 2, jnp.bfloat16, jnp.float32
    dma = pltpu.SemaphoreType.DMA
    slots = 4 * held
    vmem = pl.BlockSpec(memory_space=pltpu.VMEM)
    anywhere = pl.BlockSpec(memory_space=pl.ANY)
    return pl.pallas_call(
        functools.partial(kernel, side, depth),
        out_shape=jax.ShapeDtypeStruct((rows, feat), bf),
        in_specs=[vmem] * 3 + [anywhere] * 3,
        out_specs=vmem,
        scratch_shapes=[
            pltpu.VMEM((row_count, col_count, rows, feat), bf),
            pltpu.VMEM((col_count, rows, LANES), ff),
            pltpu.VMEM((slots, feat, width), bf),
            pltpu.VMEM((held * width, dim), bf),
            pltpu.VMEM((2 * held, col_count * rows, width), ff),
            pltpu.VMEM((col_count * rows, held * width), bf),
            pltpu.VMEM((row_count, col_count, rows, feat), bf),
            pltpu.VMEM((row_count, depth, rows, feat), bf),
            pltpu.VMEM((f, f, depth, half, feat), bf),
            pltpu.VMEM((f, f, depth, half, feat), bf),
            pltpu.VMEM((f, depth, rows, feat), bf),
            pltpu.VMEM((f, depth, rows, feat), bf),
            pltpu.VMEM((depth - 1, rows, feat), bf),
        ]
        + [dma((depth,))] * 6
        + [dma((f, depth))] * 4
        + [dma((f, f, depth))] * 4
        + [dma((side, side, depth))] * 2
        + [dma((slots,)), dma((held,)), dma]
        + [dma((side, side))] * 2
        + [dma((f, f, depth))] * 4
        + [dma((f, depth))] * 4
        + [dma((depth,))] * 2,
        compiler_params=pltpu.CompilerParams(
            collective_id=0, has_side_effects=True, vmem_limit_bytes=67043328
        ),
    )(tokens, routes, gates, w_gate, w_up, w_down)


def collectives(tokens, routes, gates, w_gate, w_up, w_down):
    held = w_gate.shape[0]
    expert_count = held * lax.axis_size("col")
    ids = jnp.arange(expert_count, dtype=jnp.int32)
    dense = jnp.sum(
        jnp.where(routes[:, :, None] == ids[None, None, :], gates[:, :, None], 0.0), axis=1
    )
    dense = lax.all_gather(dense, "col", axis=0, tiled=True)
    mine = lax.dynamic_slice_in_dim(dense, lax.axis_index("col") * held, held, axis=1)
    whole = lax.all_gather(tokens, "col", axis=0, tiled=True)
    whole = lax.all_gather(whole, "row", axis=1, tiled=True)
    gate_act = jnp.einsum("td,edf->etf", whole, w_gate, preferred_element_type=jnp.float32)
    up_act = jnp.einsum("td,edf->etf", whole, w_up, preferred_element_type=jnp.float32)
    hidden = jax.nn.silu(gate_act) * up_act * mine.T[:, :, None]
    total = jnp.einsum(
        "etf,efd->td", hidden.astype(jnp.bfloat16), w_down, preferred_element_type=jnp.float32
    ).astype(jnp.bfloat16)
    total = lax.psum_scatter(total, "row", scatter_dimension=1, tiled=True)
    return lax.psum_scatter(total, "col", scatter_dimension=0, tiled=True)


def shards(tokens, routes, gates, w_gate, w_up, w_down):
    row_count, col_count = lax.axis_size("row"), lax.axis_size("col")
    depth = col_count // 2
    fits = (
        tokens.shape[1] % LANES == 0
        and math.isqrt(row_count) ** 2 == row_count
        and row_count & (row_count - 1) == 0
        and depth >= 2
        and depth & (depth - 1) == 0
        and w_gate.shape[0] * col_count <= LANES
    )
    body = one_kernel if fits else collectives
    return body(tokens, routes, gates, w_gate, w_up, w_down)


def solution(mesh):
    return jax.shard_map(
        shards,
        mesh=mesh,
        in_specs=(
            P("col", "row"),
            P("col", None),
            P("col", None),
            P("col", None, "row"),
            P("col", None, "row"),
            P("col", "row", None),
        ),
        out_specs=P("col", "row"),
        check_vma=False,
    )
```

time: 384 us -> 103 us (0.27)
  waiting for transfers between devices: 239 us -> 0 us
  Pallas kernels: 0 us -> 98.2 us
  blocking collectives: 59.4 us -> 0 us
  matrix products: 36.3 us -> 0 us
  local copies, waits for them, and re-layouts: 24.8 us -> 4.4 us
  between operations: 13.5 us -> 0.01 us
  other arithmetic: 5.83 us -> 0 us
  starting transfers between devices: 4.96 us -> 0 us
    pallas_call x0 -> x1, Pallas kernels: none -> 98.2 us  [one_kernel(): pl.pallas_call(functools.partial(kernel, side, depth), out_shape=jax.Shap...]
    reduce_scatter x1 -> x0, waiting for transfers between devices: 92.9 us -> none  [shards(): lax.psum_scatter(term_sum.astype(jnp.bfloat16), 'row', scatter_dimension=...]
    all_gather x1 -> x0, waiting for transfers between devices: 92.9 us -> none  [shards(): piece = lax.all_gather(arrived, 'row', axis=2, tiled=True)]
    all_to_all x1 -> x0, blocking collectives: 59.4 us -> none  [shards(): lax.all_to_all(outgoing, 'col', split_axis=0, concat_axis=1, tiled=True)]
    all_to_all x1 -> x0, waiting for transfers between devices: 53.2 us -> none  [shards(): lax.all_to_all(result, 'col', split_axis=1, concat_axis=0, tiled=True)]
    dot_general x3 -> x0, matrix products: 36.3 us -> none  [the longest x1 12.7 us: shards(): jnp.einsum('erd,edf->erf', piece, w_up, preferred_element_type=jnp.float32)]
    scatter x1 -> x0, local copies, waits for them, and re-layouts: 9.86 us -> none  [shards(): outgoing.at[target].set(tokens[owner_rows])]
    reduce_scatter x1 -> x0, local copies, waits for them, and re-layouts: 5.39 us -> none  [shards(): lax.psum_scatter(term_sum.astype(jnp.bfloat16), 'row', scatter_dimension=...]
  transfers between devices with their start and end apart: 3 -> 0, of which waited for: 3 -> 0; matrix products, arithmetic and copies ran while one was open for 0% -> 0% of each run, Pallas kernels for 0% -> 0%
where the time goes in v1:
time: 103 us
  Pallas kernels  98.2 us (95%)
  local copies, waits for them, and re-layouts  4.4 us (4%)
    pallas_call x1, Pallas kernels, one_kernel(): pl.pallas_call(functools.partial(kernel, side, depth), out_shape=jax.Shap...  98.2 us
    unnamed x3, local copies, waits for them, and re-layouts  4.4 us

profile of v1, /device:TPU:0, one launch (start us, length us, event | category | flops | bytes accessed | tf_op | source)
XLA Modules:
  0.0 102.6 jit_solution(7477917823381400832)
XLA Ops:
  0.0 1.4 %copy.7.routes = s32[64,8]{1,0:T(8,128)} copy(s32[64,8]{0,1:T(8,128)} %param.7) | data formatting | bytes 4096 | tf_op args[1]
  1.4 1.4 %copy.8.gates = f32[64,8]{1,0:T(8,128)} copy(f32[64,8]{0,1:T(8,128)} %param.8) | data formatting | bytes 4096 | tf_op args[2]
  2.8 98.2 %shard_map.64 = bf16[64,1792]{1,0:T(8,128)(2,1)} custom-call(bf16[64,1792]{1,0:T(8,128)(2,1)} %tokens.1, s32[64,8]{1,0:T(8,128)} %copy.7.routes, f32[64,8]{1,0:T(8,128)} %copy.8.gates, bf16[2,7168,512]{2,1,0:T(8,128)(2,1)} %w_gate.1, bf16[2,7168,512]{2,1,0:T(8,128)(2,1)} %w_up.1, bf16[2,512,7168]{2,1,0:T(8,128)(2,1)} %w_down.1), custom_call_target="tpu_custom_call" | custom-call | tf_op jit(solution)/shard_map/pallas_call | solution.py:324
  101.0 1.6 %copy.10 = bf16[64,1792]{1,0:T(8,128)(2,1)} copy(bf16[64,1792]{1,0:T(8,128)(2,1)} %shard_map.64) | data formatting | bytes 458752

commit v2 on v1

--- a/solution.py
+++ b/solution.py
@@ -41,7 +41,15 @@
         return flip(yy, dy) * side + flip(xx, dx)
 
     def spot(j, plane=None):
-        return (core if plane is None else plane) * depth + flip(zz, j)
+        level = flip(zz, j)
+        plane = core if plane is None else plane
+        return lax.div(level, 2) * 4 + plane * 2 + lax.rem(level, 2)
+
+    def band(p):
+        return flip(lax.div(zz, 2), p)
+
+    def band_rows(p):
+        return pl.ds(pl.multiple_of(band(p) * (4 * rows), 4 * rows), 4 * rows)
 
     partner = (row, zz * 2 + 1 - core)
 
@@ -70,15 +78,18 @@
     def arrive(ref, ss, rs):
         copy_of(ref, ref, ss, rs, partner).wait_recv()
 
-    order = [(dy, dx) for dy in range(side) for dx in range(side)]
+    back = [(v, d) for v in far for d in far]
+    sides = [(0, d) for d in far] + [(d, 0) for d in far]
+    order = [(0, 0)] + sides + back
+    bands = depth // 2
     per = 2 * held
     slots = w_buf.shape[0]
-    units = len(order) * per
+    units = bands * len(order) * per
 
     def fetch(u):
         s, i = divmod(u, per)
         e, m = divmod(i, 2)
-        start = pl.multiple_of(row_of(*order[s]) * feat, LANES)
+        start = pl.multiple_of(row_of(*order[s % len(order)]) * feat, LANES)
         return pltpu.make_async_copy(
             (w_up if m else w_gate).at[e, pl.ds(start, feat), :],
             w_buf.at[u % slots],
@@ -91,10 +102,11 @@
     own.start()
 
     lane = lax.broadcasted_iota(jnp.int32, (rows, LANES), 1)
-    dense = jnp.zeros((rows, LANES), jnp.float32)
-    for k in range(routes.shape[1]):
-        dense = dense + jnp.where(lane == routes[:, k : k + 1], gates[:, k : k + 1], 0.0)
-    g_all[spot(0)] = dense
+    line = lax.broadcasted_iota(jnp.int32, (LANES, rows), 0)
+    dense = jnp.zeros((LANES, rows), jnp.float32)
+    for k in range(routes.shape[0]):
+        dense = dense + jnp.where(line == routes[k : k + 1, :], gates[k : k + 1, :], 0.0)
+    g_all[spot(0)] = dense.T
 
     barrier = pltpu.get_barrier_semaphore()
     peers = [partner] + [x_dev(d) for d in far] + [y_dev(d) for d in far]
@@ -107,19 +119,18 @@
     for d in far:
         send(tokens, mine, x_s.at[d - 1, 0], x_r.at[d - 1, 0], x_dev(d))
         send(tokens, mine, y_s.at[d - 1, 0], y_r.at[d - 1, 0], y_dev(d))
+    send(tokens, mine, p_s.at[0, 0, 0], p_r.at[0, 0, 0], partner)
+    own_gates = g_all.at[spot(0)]
     for j in levels[1:]:
         send(tokens, mine, z_s.at[j], z_r.at[j], z_dev(j))
-    send(tokens, mine, p_s.at[0, 0, 0], p_r.at[0, 0, 0], partner)
-    for j in levels[1:]:
-        send(g_all.at[spot(0)], g_all.at[spot(0)], gz_s.at[j], gz_r.at[j], z_dev(j))
-    send(g_all.at[spot(0)], g_all.at[spot(0)], gp_s.at[0], gp_r.at[0], partner)
+        send(own_gates, own_gates, gz_s.at[j], gz_r.at[j], z_dev(j))
+    send(own_gates, own_gates, gp_s.at[0], gp_r.at[0], partner)
     downs = [
         pltpu.make_async_copy(w_down.at[e], wd.at[pl.ds(e * width, width), :], wd_sem.at[e])
         for e in range(held)
     ]
     for down in downs:
         down.start()
-    acc[...] = jnp.zeros_like(acc)
     own.wait()
 
     def block(dy, dx, j):
@@ -136,6 +147,9 @@
             send(ref, ref, x_s.at[d - 1, j], x_r.at[d - 1, j], x_dev(d))
             send(ref, ref, y_s.at[d - 1, j], y_r.at[d - 1, j], y_dev(d))
         share(0, 0, j)
+        ref = g_all.at[spot(j)]
+        arrive(ref, gz_s.at[j], gz_r.at[j])
+        send(ref, ref, gp_s.at[j], gp_r.at[j], partner)
 
     def xy_event(j):
         for d in far:
@@ -161,82 +175,60 @@
                 arrive(ref.at[pl.ds(half, half)], dl_s.at[at], dl_r.at[at])
                 share(v, d, j)
 
-    def gate_event(j):
-        ref = g_all.at[spot(j)]
-        arrive(ref, gz_s.at[j], gz_r.at[j])
-        send(ref, ref, gp_s.at[j], gp_r.at[j], partner)
-
-    def ready(dy, dx):
-        for j in levels:
+    def multiply(p, s):
+        dy, dx = order[s]
+        for j in (2 * p, 2 * p + 1):
             arrive(
                 x_all.at[row_of(dy, dx), spot(j, 1 - core)], p_s.at[dy, dx, j], p_r.at[dy, dx, j]
             )
-
-    def multiply(u):
-        s, i = divmod(u, per)
-        fetch(u).wait()
-        left = x_all[row_of(*order[s])].reshape(2 * depth * rows, feat)
-        acc[i] += jnp.dot(left, w_buf[u % slots], preferred_element_type=jnp.float32)
-        if u + slots < units:
-            fetch(u + slots).start()
-
-    events = []
-    for j in range(1, depth):
-        events.append(functools.partial(z_event, j))
-        events.append(functools.partial(xy_event, j - 1))
-        if j >= 2:
-            events.append(functools.partial(diag_event, j - 2))
-    for event in events:
-        event()
-    for j in levels[1:]:
-        gate_event(j)
-    late = [functools.partial(xy_event, depth - 1)]
-    late += [functools.partial(diag_event, j) for j in range(max(depth - 2, 0), depth)]
-    stand = {per // 2: late[:1], 2 * per: late[1:2], 2 * per + per // 2: late[2:3]}
-    ready(0, 0)
-    for u in range(units):
-        for event in stand.get(u, []):
-            event()
-        if u % per == 0 and u:
-            ready(*order[u // per])
-        multiply(u)
-
-    for j in levels:
-        arrive(g_all.at[spot(j, 1 - core)], gp_s.at[j], gp_r.at[j])
-
-    def activate(b, _):
-        at = pl.ds(pl.multiple_of(b * rows, rows), rows)
-        for e in range(held):
-            weight = jnp.sum(
-                jnp.where(lane == col * held + e, g_all[b], 0.0), axis=1, keepdims=True
-            )
-            a, u = acc[2 * e, at, :], acc[2 * e + 1, at, :]
-            value = a / (1.0 + jnp.exp(-a)) * u * weight
-            hid[at, e * width : (e + 1) * width] = value.astype(jnp.bfloat16)
-        return 0
-
-    lax.fori_loop(0, 2 * depth, activate, 0)
-    for down in downs:
-        down.wait()
-
-    def project(dy, dx, plane):
+        for i in range(per):
+            u = (p * len(order) + s) * per + i
+            fetch(u).wait()
+            left = x_all[row_of(dy, dx), pl.ds(band(p) * 4, 4)].reshape(4 * rows, feat)
+            value = jnp.dot(left, w_buf[u % slots], preferred_element_type=jnp.float32)
+            if s:
+                acc[i, band_rows(p), :] += value
+            else:
+                acc[i, band_rows(p), :] = value
+            if u + slots < units:
+                fetch(u + slots).start()
+
+    def activate(p):
+        for j in (2 * p, 2 * p + 1):
+            arrive(g_all.at[spot(j, 1 - core)], gp_s.at[j], gp_r.at[j])
+
+        def step(n, _):
+            b = band(p) * 4 + n
+            at = pl.ds(pl.multiple_of(b * rows, rows), rows)
+            for e in range(held):
+                weight = jnp.sum(
+                    jnp.where(lane == col * held + e, g_all[b], 0.0), axis=1, keepdims=True
+                )
+                a, u = acc[2 * e, at, :], acc[2 * e + 1, at, :]
+                value = a / (1.0 + jnp.exp(-a)) * u * weight
+                hid[at, e * width : (e + 1) * width] = value.astype(jnp.bfloat16)
+            return 0
+
+        lax.fori_loop(0, 4, step, 0)
+        if p == 0:
+            for down in downs:
+                down.wait()
+
+    def swapped(dy, dx, p):
+        return pair.at[row_of(dy, dx), pl.ds(band(p) * 2, 2)]
+
+    def project(dy, dx, p):
         rid = row_of(dy, dx)
-        at = pl.ds(pl.multiple_of(plane * (depth * rows), rows), depth * rows)
         cols = pl.ds(pl.multiple_of(rid * feat, LANES), feat)
-        value = jnp.dot(hid[at, :], wd[:, cols], preferred_element_type=jnp.float32)
-        part[rid, pl.ds(plane * depth, depth)] = value.astype(jnp.bfloat16).reshape(
-            depth, rows, feat
+        value = jnp.dot(hid[band_rows(p), :], wd[:, cols], preferred_element_type=jnp.float32)
+        part[rid, pl.ds(band(p) * 4, 4)] = value.astype(jnp.bfloat16).reshape(4, rows, feat)
+        send(
+            part.at[rid, pl.ds(band(p) * 4 + (1 - core) * 2, 2)], swapped(dy, dx, p),
+            q_s.at[dy, dx, p], q_r.at[dy, dx, p], partner,
         )
 
-    def swap(dy, dx):
-        rid = row_of(dy, dx)
-        send(
-            part.at[rid, pl.ds((1 - core) * depth, depth)], pair.at[rid],
-            q_s.at[dy, dx], q_r.at[dy, dx], partner,
-        )
-
-    def paired(dy, dx):
-        arrive(pair.at[row_of(dy, dx)], q_s.at[dy, dx], q_r.at[dy, dx])
+    def paired(dy, dx, p):
+        arrive(swapped(dy, dx, p), q_s.at[dy, dx, p], q_r.at[dy, dx, p])
 
     def f32(value):
         return value.astype(jnp.float32)
@@ -245,31 +237,52 @@
         rid = row_of(dy, dx)
         return f32(part[rid, spot(j)]) + f32(pair[rid, flip(zz, j)])
 
-    back = [(v, d) for v in far for d in far]
-    sides = [(0, d) for d in far] + [(d, 0) for d in far]
     falling = list(reversed(levels))
 
-    def diag_out():
+    def diag_out(p):
         for v, d in back:
-            paired(v, d)
-            for j in falling:
+            paired(v, d, p)
+            for j in (2 * p + 1, 2 * p):
                 ref = part.at[row_of(v, d), spot(j)]
                 part[row_of(v, d), spot(j)] = both(v, d, j).astype(jnp.bfloat16)
                 at = (v - 1, d - 1, j)
                 send(ref.at[pl.ds(0, half)], dx_in.at[at], ou_s.at[at], ou_r.at[at], x_dev(d))
                 send(ref.at[pl.ds(half, half)], dy_in.at[at], ol_s.at[at], ol_r.at[at], y_dev(v))
 
-    todo = back + sides + [(0, 0)]
-    for n, (dy, dx) in enumerate(todo):
-        project(dy, dx, 1 - core)
-        swap(dy, dx)
-        if n == len(back):
-            diag_out()
-        project(dy, dx, core)
-
-    for dy, dx in sides:
-        paired(dy, dx)
+    near = 1 + len(sides)
+    z_event(1)
+    for p in range(bands):
+        more = p + 1 < bands
+        multiply(p, 0)
+        if p == 0:
+            xy_event(0)
+        xy_event(2 * p + 1)
+        for s in range(1, near):
+            multiply(p, s)
+            if more and s == 1:
+                z_event(2 * p + 2)
+        diag_event(2 * p)
+        if p:
+            diag_out(p - 1)
+        diag_event(2 * p + 1)
+        for s in range(near, len(order)):
+            multiply(p, s)
+        if more:
+            z_event(2 * p + 3)
+        activate(p)
+        for dy, dx in back:
+            project(dy, dx, p)
+        if more:
+            xy_event(2 * p + 2)
+        for n, (dy, dx) in enumerate(sides + [(0, 0)]):
+            project(dy, dx, p)
+            if not more and n == 0:
+                diag_out(p)
+
     for j in falling:
+        if j % 2:
+            for dy, dx in sides:
+                paired(dy, dx, j // 2)
         for d in far:
             total = both(0, d, j)
             top, low = total[:half], total[half:]
@@ -292,8 +305,9 @@
             ref[pl.ds(0, half), :] = top.astype(jnp.bfloat16)
             ref[pl.ds(half, half), :] = low.astype(jnp.bfloat16)
             send(ref, ry_in.at[v - 1, j], ry_s.at[v - 1, j], ry_r.at[v - 1, j], y_dev(v))
-    paired(0, 0)
     for j in falling:
+        if j % 2:
+            paired(0, 0, j // 2)
         total = both(0, 0, j)
         for d in far:
             arrive(rx_in.at[d - 1, j], rx_s.at[d - 1, j], rx_r.at[d - 1, j])
@@ -346,14 +360,14 @@
         + [dma((f, f, depth))] * 4
         + [dma((side, side, depth))] * 2
         + [dma((slots,)), dma((held,)), dma]
-        + [dma((side, side))] * 2
+        + [dma((side, side, depth // 2))] * 2
         + [dma((f, f, depth))] * 4
         + [dma((f, depth))] * 4
         + [dma((depth,))] * 2,
         compiler_params=pltpu.CompilerParams(
             collective_id=0, has_side_effects=True, vmem_limit_bytes=67043328
         ),
-    )(tokens, routes, gates, w_gate, w_up, w_down)
+    )(tokens, routes.T, gates.T, w_gate, w_up, w_down)
 
 
 def collectives(tokens, routes, gates, w_gate, w_up, w_down):

time: 103 us -> 88.7 us (0.86)
  Pallas kernels: 98.2 us -> 86.9 us
  local copies, waits for them, and re-layouts: 4.4 us -> 1.64 us
    pallas_call x1, Pallas kernels: 98.2 us -> 86.9 us  [one_kernel(): pl.pallas_call(functools.partial(kernel, side, depth), out_shape=jax.Shap...]
    unnamed x3 -> x1, local copies, waits for them, and re-layouts: 4.4 us -> 1.64 us
where the time goes in v2:
time: 88.7 us; the launch traced here: 88.6 us
  Pallas kernels  86.9 us (98%)
  local copies, waits for them, and re-layouts  1.64 us (2%)
    pallas_call x1, Pallas kernels, one_kernel(): pl.pallas_call(functools.partial(kernel, side, depth), out_shape=jax.Shap...  86.9 us

profile of v2, /device:TPU:0, one launch (start us, length us, event | category | flops | bytes accessed | tf_op | source)
XLA Modules:
  0.0 88.6 jit_solution(1852433093883400649)
XLA Ops:
  0.0 86.9 %shard_map.64 = bf16[64,1792]{1,0:T(8,128)(2,1)} custom-call(bf16[64,1792]{1,0:T(8,128)(2,1)} %tokens.1, s32[8,64]{1,0:T(8,128)} %bitcast.2, f32[8,64]{1,0:T(8,128)} %bitcast.3, bf16[2,7168,512]{2,1,0:T(8,128)(2,1)} %w_gate.1, bf16[2,7168,512]{2,1,0:T(8,128)(2,1)} %w_up.1, bf16[2,512,7168]{2,1,0:T(8,128)(2,1)} %w_down.1), custom_call_target="tpu_custom_call" | custom-call | tf_op jit(solution)/shard_map/pallas_call | solution.py:338
  86.9 1.6 %copy.8 = bf16[64,1792]{1,0:T(8,128)(2,1)} copy(bf16[64,1792]{1,0:T(8,128)(2,1)} %shard_map.64) | data formatting | bytes 458752
